TPU v7x, 256 devices: a whole 4x4x8 slice. The times are simulated.
256 devices in a mesh: src: 8 (over y, core), tp: 16 (over x, z_hi), row: 2 (over z_lo).
Axes of the slice: x: 4, y: 4, z: 8 (z_hi: 4, z_lo: 2; z = z_hi * 2 + z_lo), core: 2. Of those that a mesh axis runs over, the one named last changes fastest.
Arguments:
- tokens: bfloat16 [8, 256, 8192], P('src', 'tp', 'row'), may hold values from -6 to 6
- coefficients: float32 [8, 8], replicated, may hold values from -2 to 2
- gate_weights: bfloat16 [8, 8192, 4096], P('src', 'row', 'tp'), may hold values from -0.0625 to 0.0625
- up_weights: bfloat16 [8, 8192, 4096], P('src', 'row', 'tp'), may hold values from -0.0625 to 0.0625
Outputs:
- hidden: bfloat16 [8, 256, 4096], P('src', 'row', 'tp')
All inputs are finite; a program needn't handle non-finite values.
Results may differ from a plain program's by a relative error of at most 0.0013.
Values may be sent and summed in bfloat16 or wider, within the bound.
A program may use at most 64 MiB of HBM per device.

v0:
```python
import jax
import jax.numpy as jnp
from jax import lax
from jax.sharding import PartitionSpec as P


def split_up(array, dim, devices):
    shape = array.shape
    tiles = array.reshape(*shape[:dim], devices, shape[dim] // devices, *shape[dim + 1 :])
    return jnp.moveaxis(tiles, dim, 0)


def sent_and_summed(array, axis, dim):
    tiles = split_up(array, dim, lax.axis_size(axis))
    arrived = lax.all_to_all(tiles, axis, split_axis=0, concat_axis=0, tiled=True)
    return arrived.sum(axis=0)


def shards(tokens, coefficients, gate_weights, up_weights):
    local_rows = tokens.shape[1]
    half_width = tokens.shape[2]
    candidates = coefficients.shape[0]
    sources = coefficients.shape[1]
    per_candidate = local_rows * lax.axis_size("tp")
    out_rows = per_candidate // lax.axis_size("row")
    own_source = lax.axis_index("src")
    picked = (jnp.arange(sources, dtype=jnp.int32) == own_source).astype(jnp.float32)
    own_factors = jnp.sum(coefficients * picked[None, :], axis=1)
    gate_local = gate_weights[0]
    up_local = up_weights[0]
    hidden_width = gate_local.shape[1]
    flat_tokens = tokens.reshape(local_rows, half_width)
    row_block = lax.all_gather(flat_tokens, ("src", "tp"), axis=0, tiled=True)
    row_count = row_block.shape[0]
    owner_ids = jnp.arange(row_count, dtype=jnp.int32) // per_candidate
    one_hot = (owner_ids[:, None] == jnp.arange(candidates, dtype=jnp.int32)[None, :]).astype(
        jnp.float32
    )
    factor = jnp.sum(one_hot * own_factors[None, :], axis=1)[:, None]
    gate_part = jnp.dot(row_block, gate_local, preferred_element_type=jnp.float32)
    up_part = jnp.dot(row_block, up_local, preferred_element_type=jnp.float32)
    collected = jnp.concatenate((gate_part, up_part), axis=1) * factor
    summed = sent_and_summed(collected, ("src", "row"), 0)
    hidden = (jax.nn.silu(summed[:, :hidden_width]) * summed[:, hidden_width:]).astype(jnp.bfloat16)
    return hidden.reshape(1, out_rows, hidden_width)


def solution(mesh):
    return jax.shard_map(
        shards,
        mesh=mesh,
        in_specs=(P("src", "tp", "row"), P(), P("src", "row", "tp"), P("src", "row", "tp")),
        out_specs=P("src", "row", "tp"),
        check_vma=False,
    )
```

profile of v0, /device:TPU:1, one launch (start us, length us, event | category | flops | bytes accessed | tf_op | source)
XLA Modules:
  0.0 212.2 jit_solution(2710372214216165005)
XLA Ops:
  6.5 0.0 copy-start
  6.5 0.0 all-gather.3.cloned.1.call-start
  6.5 0.7 all-gather.3.cloned.1.call-update
  7.3 0.8 multiply_reduce_fusion
  8.1 0.1 select_reduce_fusion
  8.2 123.5 %all-gather.3.cloned.1.call-done = bf16[1,2048,4096]{2,1,0:T(8,128)(2,1)} async-done(((bf16[1,16,4096]{2,1,0:T(8,128)(2,1)}), bf16[1,2048,4096]{2,1,0:T(8,128)(2,1)}) %all-gather.3.cloned.1.call-update) | async-done | bytes 16777232 | tf_op jit(solution)/shard_map/all_gather | solution.py:33
  131.7 0.0 copy-done
  131.7 0.0 copy-start.1
  131.7 0.0 copy-start.2
  131.7 8.3 %fusion = f32[16,128,256]{2,1,0:T(8,128)S(1)} fusion(bf16[16,128,4096]{2,1,0:T(8,128)(2,1)} %bitcast.15, bf16[1,4096,256]{2,1,0:T(8,128)(2,1)S(1)} %copy-done), kind=kOutput, calls=%fused_computation.1 | convolution fusion | flops 4294967296 | bytes 20971520 | tf_op jit(solution)/shard_map/dot_general | solution.py:41
  140.0 2.3 %copy-done.1 = bf16[1,2048,4096]{2,1,0:T(8,128)(2,1)S(1)} copy-done((bf16[1,2048,4096]{2,1,0:T(8,128)(2,1)S(1)}, bf16[1,2048,4096]{2,1,0:T(8,128)(2,1)}, u32[]{:S(2)}) %copy-start.1) | copy-done | bytes 16777240
  142.3 0.6 copy-done.2
  142.9 4.9 %fusion.2 = f32[16,128,256]{2,1,0:T(8,128)S(1)} fusion(bf16[16,128,4096]{2,1,0:T(8,128)(2,1)S(1)} %bitcast.16, bf16[1,4096,256]{2,1,0:T(8,128)(2,1)S(1)} %copy-done.2), kind=kOutput, calls=%fused_computation.3 | convolution fusion | flops 4294967296 | bytes 20971520 | tf_op jit(solution)/shard_map/dot_general | solution.py:40
  147.8 0.4 maximum_multiply_fusion
  148.2 53.9 %all_to_all.5 = f32[16,128,512]{2,1,0:T(8,128)} all-to-all(f32[16,128,512]{2,1,0:T(8,128)S(1)} %maximum_multiply_fusion), channel_id=1, replica_groups=mesh['src'=8,'tp'=16,'row'=2] {'src','row'}, dimensions={0} | all-to-all | bytes 8388608 | tf_op jit(solution)/shard_map/all_to_all | solution.py:15
  202.0 2.6 %reduce_sum.29 = f32[128,512]{1,0:T(8,128)S(1)} reduce(f32[16,128,512]{2,1,0:T(8,128)} %all_to_all.5, f32[]{:T(128)} %constant.28.clone.1), dimensions={0}, to_apply=%region_2.3 | reduce | flops 983040 | bytes 4456452 | tf_op jit(solution)/shard_map/reduce_sum | solution.py:16
  204.7 0.7 fusion.5
  (2 shorter events, 0.0 us)
Async XLA Ops:
  6.5 125.2 %copy-start = (bf16[1,4096,256]{2,1,0:T(8,128)(2,1)S(1)}, bf16[1,4096,256]{2,1,0:T(8,128)(2,1)}, u32[]{:S(2)}) copy-start(bf16[1,4096,256]{2,1,0:T(8,128)(2,1)} %param.7) | copy-start | bytes 6291460
  6.5 125.2 %all-gather.3.cloned.1.call-start = ((), (), s32[]{:S(2)}) async-start(), calls=%async_computation.1 | async-start | bytes 16908288 | tf_op jit(solution)/shard_map/all_gather | solution.py:33
  131.7 10.5 %copy-start.1 = (bf16[1,2048,4096]{2,1,0:T(8,128)(2,1)S(1)}, bf16[1,2048,4096]{2,1,0:T(8,128)(2,1)}, u32[]{:S(2)}) copy-start(bf16[1,2048,4096]{2,1,0:T(8,128)(2,1)} %all-gather.3.cloned.1.call-done) | copy-start | bytes 50331652
  131.7 11.1 %copy-start.2 = (bf16[1,4096,256]{2,1,0:T(8,128)(2,1)S(1)}, bf16[1,4096,256]{2,1,0:T(8,128)(2,1)}, u32[]{:S(2)}) copy-start(bf16[1,4096,256]{2,1,0:T(8,128)(2,1)} %param.6) | copy-start | bytes 6291460
Sparse Core Ops, SparseCore 0:
  10.9 120.7 all-gather.2
where the time goes:
time: 212 us
  waiting for transfers between devices  124 us (58%)
  blocking collectives  53.9 us (25%)
  between operations  13.4 us (6%)
  matrix products  13.2 us (6%)
  other arithmetic  4.6 us (2%)
  local copies, waits for them, and re-layouts  2.86 us (1%)
    all_gather x1, waiting for transfers between devices, shards(): row_block = lax.all_gather(flat_tokens, ('src', 'tp'), axis=0, tiled=True)  124 us
    all_to_all x1, blocking collectives, sent_and_summed(): lax.all_to_all(tiles, axis, split_axis=0, concat_axis=0, tiled=True)  53.9 us
    dot_general x1, matrix products, shards(): up_part = jnp.dot(row_block, up_local, preferred_element_type=jnp.float32)  8.28 us
    dot_general x1, matrix products, shards(): jnp.dot(row_block, gate_local, preferred_element_type=jnp.float32)  4.9 us
  transfers between devices with their start and end apart: 1, of which 1 were waited for; matrix products, arithmetic and copies ran while one was open for 0% of the time, Pallas kernels for 0%

commit v1 on v0

--- a/solution.py
+++ b/solution.py
@@ -30,7 +30,10 @@
     up_local = up_weights[0]
     hidden_width = gate_local.shape[1]
     flat_tokens = tokens.reshape(local_rows, half_width)
-    row_block = lax.all_gather(flat_tokens, ("src", "tp"), axis=0, tiled=True)
+    now = lax.all_to_all(
+        jnp.stack(lax.axis_size(("src", "tp")) * [flat_tokens], axis=0), ("src", "tp"), 0, 0
+    )
+    row_block = jnp.concatenate(now, axis=0)
     row_count = row_block.shape[0]
     owner_ids = jnp.arange(row_count, dtype=jnp.int32) // per_candidate
     one_hot = (owner_ids[:, None] == jnp.arange(candidates, dtype=jnp.int32)[None, :]).astype(

time: 212 us -> 474 us (2.24); the launches traced: 212 us -> 468 us
  waiting for transfers between devices: 124 us -> 370 us
  starting transfers between devices: 0.01 us -> 17 us
  between operations: 13.4 us -> 0.08 us
    all_to_all x0 -> x1, waiting for transfers between devices: none -> 370 us  [shards(): lax.all_to_all(jnp.stack(lax.axis_size(('src', 'tp')) * [flat_tokens], ax...]
    all_gather x1 -> x0, waiting for transfers between devices: 124 us -> none  [shards(): row_block = lax.all_gather(flat_tokens, ('src', 'tp'), axis=0, tiled=True)]
    all_to_all x0 -> x1, starting transfers between devices: none -> 17 us  [shards(): lax.all_to_all(jnp.stack(lax.axis_size(('src', 'tp')) * [flat_tokens], ax...]
    another operation x0 -> x1, local copies, waits for them, and re-layouts: none -> 6.86 us  [shards(): jnp.stack(lax.axis_size(('src', 'tp')) * [flat_tokens], axis=0)]
where the time goes in v1:
time: 474 us; the launch traced here: 468 us
  waiting for transfers between devices  370 us (78%)
  blocking collectives  53.4 us (11%)
  starting transfers between devices  17 us (4%)
  matrix products  16.4 us (3%)
  local copies, waits for them, and re-layouts  6.88 us (1%)
    all_to_all x1, waiting for transfers between devices, shards(): lax.all_to_all(jnp.stack(lax.axis_size(('src', 'tp')) * [flat_tokens], ax...  370 us
    all_to_all x1, blocking collectives, sent_and_summed(): lax.all_to_all(tiles, axis, split_axis=0, concat_axis=0, tiled=True)  53.4 us
    all_to_all x1, starting transfers between devices, shards(): lax.all_to_all(jnp.stack(lax.axis_size(('src', 'tp')) * [flat_tokens], ax...  17 us
  transfers between devices with their start and end apart: 1, of which 1 were waited for; matrix products, arithmetic and copies ran while one was open for 0% of the time, Pallas kernels for 0%

profile of v1, /device:TPU:1, one launch (start us, length us, event | category | flops | bytes accessed | tf_op | source)
XLA Modules:
  0.0 467.7 jit_solution(11336651642070040880)
XLA Ops:
  0.0 0.0 copy-start
  0.0 6.9 %stack.3 = bf16[128,16,4096]{2,1,0:T(8,128)(2,1)} broadcast(bf16[16,4096]{1,0:T(8,128)(2,1)} %bitcast.15), dimensions={1,2} | broadcast | bytes 16908288 | tf_op jit(solution)/shard_map/stack | solution.py:34
  6.9 0.0 copy-start.1
  6.9 17.0 %all-to-all-start = ((bf16[128,16,4096]{2,1,0:T(8,128)(2,1)}), bf16[128,16,4096]{2,1,0:T(8,128)(2,1)}, u32[]{:S(2)}, u32[]{:S(2)}) async-start(bf16[128,16,4096]{2,1,0:T(8,128)(2,1)} %stack.3), calls=%async_computation | async-start | bytes 33554432 | tf_op jit(solution)/shard_map/all_to_all | solution.py:33
  23.9 0.0 copy-done.1
  23.9 0.1 multiply_reduce_fusion
  24.0 0.1 select_reduce_fusion
  24.1 370.1 %all-to-all-done = bf16[128,16,4096]{2,1,0:T(8,128)(2,1)} async-done(((bf16[128,16,4096]{2,1,0:T(8,128)(2,1)}), bf16[128,16,4096]{2,1,0:T(8,128)(2,1)}, u32[]{:S(2)}, u32[]{:S(2)}) %all-to-all-start) | async-done | bytes 16777248 | tf_op jit(solution)/shard_map/all_to_all | solution.py:33
  394.2 0.0 copy-done
  394.2 0.0 copy-start.2
  394.2 8.3 %fusion = f32[16,128,256]{2,1,0:T(8,128)S(1)} fusion(bf16[16,128,4096]{2,1,0:T(8,128)(2,1)} %bitcast.1, bf16[1,4096,256]{2,1,0:T(8,128)(2,1)S(1)} %copy-done), kind=kOutput, calls=%fused_computation.1 | convolution fusion | flops 4294967296 | bytes 20971520 | tf_op jit(solution)/shard_map/dot_general | solution.py:44
  402.5 0.0 copy-done.2
  402.5 8.2 %fusion.2 = f32[16,128,256]{2,1,0:T(8,128)S(1)} fusion(bf16[16,128,4096]{2,1,0:T(8,128)(2,1)} %bitcast.1, bf16[1,4096,256]{2,1,0:T(8,128)(2,1)S(1)} %copy-done.2), kind=kOutput, calls=%fused_computation.3 | convolution fusion | flops 4294967296 | bytes 20971520 | tf_op jit(solution)/shard_map/dot_general | solution.py:43
  410.6 0.4 maximum_multiply_fusion
  411.0 53.4 %all_to_all.10 = f32[16,128,512]{2,1,0:T(8,128)} all-to-all(f32[16,128,512]{2,1,0:T(8,128)S(1)} %maximum_multiply_fusion), channel_id=1, replica_groups=mesh['src'=8,'tp'=16,'row'=2] {'src','row'}, dimensions={0} | all-to-all | bytes 8388608 | tf_op jit(solution)/shard_map/all_to_all | solution.py:15
  464.4 2.6 reduce_sum.29
  467.1 0.7 fusion.5
  (2 shorter events, 0.0 us)
Async XLA Ops:
  0.0 394.2 %copy-start = (bf16[1,4096,256]{2,1,0:T(8,128)(2,1)S(1)}, bf16[1,4096,256]{2,1,0:T(8,128)(2,1)}, u32[]{:S(2)}) copy-start(bf16[1,4096,256]{2,1,0:T(8,128)(2,1)} %param.7) | copy-start | bytes 6291460
  6.9 17.0 %copy-start.1 = (f32[8,8]{1,0:T(8,128)S(1)}, f32[8,8]{1,0:T(8,128)}, u32[]{:S(2)}) copy-start(f32[8,8]{1,0:T(8,128)} %param.5) | copy-start | bytes 772
  6.9 387.3 %all-to-all-start = ((bf16[128,16,4096]{2,1,0:T(8,128)(2,1)}), bf16[128,16,4096]{2,1,0:T(8,128)(2,1)}, u32[]{:S(2)}, u32[]{:S(2)}) async-start(bf16[128,16,4096]{2,1,0:T(8,128)(2,1)} %stack.3), calls=%async_computation | async-start | bytes 33554432 | tf_op jit(solution)/shard_map/all_to_all | solution.py:33
  394.2 8.3 %copy-start.2 = (bf16[1,4096,256]{2,1,0:T(8,128)(2,1)S(1)}, bf16[1,4096,256]{2,1,0:T(8,128)(2,1)}, u32[]{:S(2)}) copy-start(bf16[1,4096,256]{2,1,0:T(8,128)(2,1)} %param.6) | copy-start | bytes 6291460
